TPU v7x, 32 devices: a whole 2x2x4 slice. The times are simulated.
32 devices in a mesh: groups: 2 (over y), tm: 4 (over z), chan: 2 (over x), sub: 2 (over core).
Axes of the slice: x: 2, y: 2, z: 4, core: 2. Of those that a mesh axis runs over, the one named last changes fastest.
Arguments:
- traces: bfloat16 [512, 8192], P(('chan', 'sub'), ('groups', 'tm')), parts along dimension 1, may hold values from -60 to 60
- templates: bfloat16 [32, 512, 256], P('tm', ('chan', 'sub')), may hold values from -6 to 6
- channel_mask: int32 [32, 512], P('tm', ('chan', 'sub')), may hold values from 0 to 1
Outputs:
- scores: float32 [32, 8192], P(('chan', 'sub'), ('groups', 'tm')), parts along dimension 1
There are 2 independent parts, one for each index of `groups`. A program takes and returns all parts, laid end to end along the dimension named above; an argument that names none is the same for every part. Nothing has to cross between parts.
All inputs are finite; a program needn't handle non-finite values.
Results may differ from a plain program's by a relative error of at most 0.0003.
Values may be sent and summed in bfloat16 or wider, within the bound.
A program may use at most 64 MiB of HBM per device.

v0:
```python
import jax
import jax.numpy as jnp
from jax import lax
from jax.sharding import PartitionSpec as P

EPSILON = 1e-06
lag_step = 8


def shifted(x, axis, by):
    count = lax.axis_size(axis)
    return lax.ppermute(x, axis, [(i, (i + by) % count) for i in range(count)])


def window_sums(values, stride, terms_count):
    length = values.shape[1] - (terms_count - 1) * stride
    running = values[:, :length]
    for offset in range(1, terms_count):
        running = running + values[:, offset * stride : offset * stride + length]
    return running


def pad_tile(tile_data):
    return jnp.concatenate(
        [tile_data, jnp.zeros((tile_data.shape[0], lag_step), tile_data.dtype)], 1
    )


def channel_energy(extended, span_len, tile_len):
    squares = jnp.square(extended.astype(jnp.float32))
    sums_one = window_sums(squares, 1, lag_step)
    sums_two = window_sums(sums_one, lag_step, lag_step)
    sums_three = window_sums(sums_two, lag_step * lag_step, span_len // (lag_step * lag_step))
    return sums_three[:, :tile_len]


def build_frames(extended, frame_width):
    stacked = jnp.stack(
        [extended[:, offset : offset + frame_width] for offset in range(lag_step)], 1
    )
    return stacked.reshape(-1, frame_width)


def correlate(arranged, frames, tile_len, lag_blocks):
    partial_value = jnp.dot(arranged, frames, preferred_element_type=jnp.float32)
    block_rows = partial_value.shape[0] // lag_blocks
    frame_width = frames.shape[1]
    flattened = partial_value.reshape(block_rows, lag_blocks * frame_width)
    flattened = jnp.pad(flattened, ((0, 0), (0, lag_blocks * lag_step)))
    skewed = flattened.reshape(block_rows, lag_blocks, frame_width + lag_step)[:, :, :tile_len]
    return jnp.sum(skewed, axis=1)


def template_stats(arranged, mask_rows, lag_blocks):
    block_rows = arranged.shape[0] // lag_blocks
    values = arranged.astype(jnp.float32).reshape(block_rows, lag_blocks, arranged.shape[1])
    template_energy = jnp.sum(values * values, axis=(1, 2))
    active = mask_rows.astype(jnp.float32)
    return (active, template_energy, jnp.sum(active, axis=1))


def normalize(correlation, energy, template_energy, active_count, span_len):
    factor = jnp.sqrt(span_len * active_count)[:, None]
    return correlation * factor / jnp.sqrt(energy * template_energy[:, None] + EPSILON)


def place_rows(accums, updates, anchor, block_rows):
    first_row = anchor * block_rows
    return tuple(
        (
            lax.dynamic_update_slice_in_dim(stored, update, first_row, 0)
            for stored, update in zip(accums, updates)
        )
    )


def on_device(traces, templates, channel_mask):
    chan_dev = traces.shape[0]
    tile_len = traces.shape[1]
    block_rows = templates.shape[0]
    span_len = templates.shape[2]
    lag_blocks = span_len // lag_step
    frame_width = tile_len + span_len
    circle = lax.axis_size("tm")
    my_tile = lax.axis_index("tm")
    subarrays = lax.axis_size(("chan", "sub"))
    border_cols = shifted(traces[:, :span_len], "tm", -1)
    joined = jnp.concatenate([traces, border_cols], 1)
    mask_rows = channel_mask.astype(jnp.bfloat16)
    masked = templates * mask_rows[:, :, None]
    arranged = masked.reshape(block_rows, chan_dev, lag_blocks, lag_step).transpose(0, 2, 1, 3)
    arranged = arranged.reshape(block_rows * lag_blocks, chan_dev * lag_step)
    all_rows = block_rows * circle
    share_rows = all_rows // subarrays
    extended = pad_tile(joined)
    frames = build_frames(extended, frame_width)
    chan_energy = channel_energy(extended, span_len, tile_len)

    def absorb(accums, held_block, held_mask, anchor):
        active, template_energy, active_count = template_stats(held_block, held_mask, lag_blocks)
        correlation = correlate(held_block, frames, tile_len, lag_blocks)
        energy = jnp.dot(
            active, chan_energy, precision=lax.Precision.HIGHEST, preferred_element_type=jnp.float32
        )
        return place_rows(
            accums, (correlation, energy, template_energy, active_count), anchor, block_rows
        )

    zero_grid = jnp.zeros((all_rows, tile_len), jnp.float32)
    zero_rows = jnp.zeros((all_rows,), jnp.float32)
    accums = absorb((zero_grid, zero_grid, zero_rows, zero_rows), arranged, mask_rows, my_tile)

    def advance(hop_index, state_tuple):
        held_block, held_mask, stored = state_tuple
        held_block, held_mask = shifted((held_block, held_mask), "tm", 1)
        return (
            held_block,
            held_mask,
            absorb(stored, held_block, held_mask, (my_tile - hop_index) % circle),
        )

    _, _, accums = lax.fori_loop(1, circle, advance, (arranged, mask_rows, accums))
    correlation, energy, template_energy, active_count = lax.psum(accums, ("chan", "sub"))
    first_row = lax.axis_index(("chan", "sub")) * share_rows
    correlation = lax.dynamic_slice_in_dim(correlation, first_row, share_rows, 0)
    energy = lax.dynamic_slice_in_dim(energy, first_row, share_rows, 0)
    template_energy = lax.dynamic_slice_in_dim(template_energy, first_row, share_rows, 0)
    active_count = lax.dynamic_slice_in_dim(active_count, first_row, share_rows, 0)
    return normalize(correlation, energy, template_energy, active_count, span_len)


def solution(mesh):
    placed = (
        P(("chan", "sub"), ("groups", "tm")),
        P("tm", ("chan", "sub"), None),
        P("tm", ("chan", "sub")),
    )
    return jax.shard_map(
        on_device,
        mesh=mesh,
        in_specs=placed,
        out_specs=P(("chan", "sub"), ("groups", "tm")),
        check_vma=False,
    )
```

profile of v0, /device:TPU:0, one launch (start us, length us, event | category | flops | bytes accessed | tf_op | source)
XLA Modules:
  0.0 137.7 jit_solution(13104701625816900502)
XLA Ops:
  6.5 0.8 slice.100
  7.4 5.1 %collective-permute-start.2 = (bf16[128,256]{1,0:T(8,128)(2,1)S(1)}, bf16[128,256]{1,0:T(8,128)(2,1)S(1)}, u32[]{:S(2)}, u32[]{:S(2)}) collective-permute-start(bf16[128,256]{1,0:T(8,128)(2,1)S(1)} %slice.100), channel_id=1, source_target_pairs={{0,12},{4,0},{8,4},{12,8},{1,13},{5,1},{9,5},{13,9},{2,14},{6,2},{... | collective-permute-start | bytes 196616 | tf_op jit(solution)/shard_map/ppermute | solution.py:12
  12.5 0.8 convert_reduce_fusion.1
  13.3 1.3 copy.18
  14.6 0.3 multiply_reduce_fusion.1
  14.9 3.4 %copy.19 = bf16[8,32,128,8]{1,0,3,2:T(8,128)(2,1)S(1)} copy(bf16[8,32,128,8]{2,3,1,0:T(8,128)(2,1)S(1)} %get-tuple-element.313) | data formatting | bytes 1048576 | tf_op jit(solution)/shard_map/transpose | solution.py:91
  18.3 1.6 %reshape.50 = bf16[256,1024]{0,1:T(8,128)(2,1)S(1)} reshape(bf16[8,32,128,8]{1,0,3,2:T(8,128)(2,1)S(1)} %copy.19) | data formatting | bytes 1048576 | tf_op jit(solution)/shard_map/reshape | solution.py:92
  20.0 1.0 copy.21
  21.0 0.2 dynamic_update_slice.54
  21.2 0.2 dynamic_update_slice.55
  22.7 1.9 %fusion.9 = f32[256,1280]{1,0:T(8,128)S(1)} fusion(bf16[256,1024]{0,1:T(8,128)(2,1)S(1)} %reshape.50, bf16[128,8,1280]{2,0,1:T(8,128)(2,1)S(1)} %fusion.1), kind=kOutput, calls=%fused_computation.50 | convolution fusion | flops 671088640 | bytes 4456448 | tf_op jit(solution)/shard_map/dot_general | solution.py:45
  24.6 2.9 %copy.24 = bf16[128,8,1280]{2,1,0:T(8,128)(2,1)} copy(bf16[128,8,1280]{2,0,1:T(8,128)(2,1)S(1)} %fusion.1) | data formatting | bytes 5242880 | tf_op jit(solution)/shard_map/stack | solution.py:38
  27.5 0.2 reshape.52
  27.8 1.2 reshape.53
  29.2 1.4 slice_add_fusion
  30.6 1.2 slice_add_fusion.7
  31.9 0.4 fusion.10
  32.3 0.9 slice_add_fusion.14
  33.2 1.3 fusion
  34.5 63.4 %while.25 = (s32[]{:T(128)}, bf16[256,1024]{1,0:T(8,128)(2,1)S(1)}, bf16[8,128]{1,0:T(8,128)(2,1)S(1)}, f32[32,1024]{1,0:T(8,128)S(1)}, f32[32,1024]{1,0:T(8,128...) while((s32[]{:T(128)}, bf16[256,1024]{1,0:T(8,128)(2,1)S(1)}, ...), condition=%wide.region_8.9_spmd, body=%wide.region_3.8_spmd.sunk | while | flops 684713984 | bytes 17741476 | solution.py:122
  34.9 15.1 %collective-permute-done.1 = bf16[8,128]{1,0:T(8,128)(2,1)S(1)} collective-permute-done((bf16[8,128]{1,0:T(8,128)(2,1)S(1)}, bf16[8,128]{1,0:T(8,128)(2,1)S(1)}, u32[]{:S(2)}, u32[]{:S(2)}) %collective-permute-start.1) | collective-permute-done | bytes 2080 | tf_op jit(solution)/shard_map/while/body/eval_jaxpr/ppermute | solution.py:12
  50.2 0.2 dynamic_update_slice.67
  50.4 1.3 convolution_dynamic-update-slice_fusion.2
  51.8 2.6 %fusion.28 = f32[256,1280]{1,0:T(8,128)S(1)} fusion(bf16[256,1024]{1,0:T(8,128)(2,1)S(1)} %collective-permute-done, bf16[1024,1280]{1,0:T(8,128)(2,1)} %get-tuple-element.420), kind=kOutput, calls=%fused_computation.52.clone.1 | convolution fusion | flops 671088640 | bytes 4456448 | tf_op jit(solution)/shard_map/while/body/eval_jaxpr/dot_general | solution.py:45
  54.3 0.2 reshape.56
  54.7 1.2 reshape.57
  56.0 0.2 multiply_reduce_fusion.3
  56.4 0.2 dynamic_update_slice.66
  56.9 14.3 %collective-permute-done.1 = bf16[8,128]{1,0:T(8,128)(2,1)S(1)} collective-permute-done((bf16[8,128]{1,0:T(8,128)(2,1)S(1)}, bf16[8,128]{1,0:T(8,128)(2,1)S(1)}, u32[]{:S(2)}, u32[]{:S(2)}) %collective-permute-start.1) | collective-permute-done | bytes 2080 | tf_op jit(solution)/shard_map/while/body/eval_jaxpr/ppermute | solution.py:12
  71.2 0.2 dynamic_update_slice.67
  71.5 1.3 convolution_dynamic-update-slice_fusion.2
  72.8 2.6 %fusion.28 = f32[256,1280]{1,0:T(8,128)S(1)} fusion(bf16[256,1024]{1,0:T(8,128)(2,1)S(1)} %collective-permute-done, bf16[1024,1280]{1,0:T(8,128)(2,1)} %get-tuple-element.420), kind=kOutput, calls=%fused_computation.52.clone.1 | convolution fusion | flops 671088640 | bytes 4456448 | tf_op jit(solution)/shard_map/while/body/eval_jaxpr/dot_general | solution.py:45
  75.4 0.2 reshape.56
  75.8 1.2 reshape.57
  77.1 0.2 multiply_reduce_fusion.3
  77.5 0.2 dynamic_update_slice.66
  77.9 13.4 %collective-permute-done.1 = bf16[8,128]{1,0:T(8,128)(2,1)S(1)} collective-permute-done((bf16[8,128]{1,0:T(8,128)(2,1)S(1)}, bf16[8,128]{1,0:T(8,128)(2,1)S(1)}, u32[]{:S(2)}, u32[]{:S(2)}) %collective-permute-start.1) | collective-permute-done | bytes 2080 | tf_op jit(solution)/shard_map/while/body/eval_jaxpr/ppermute | solution.py:12
  91.5 0.2 dynamic_update_slice.67
  91.7 1.3 convolution_dynamic-update-slice_fusion.2
  93.0 2.6 %fusion.28 = f32[256,1280]{1,0:T(8,128)S(1)} fusion(bf16[256,1024]{1,0:T(8,128)(2,1)S(1)} %collective-permute-done, bf16[1024,1280]{1,0:T(8,128)(2,1)} %get-tuple-element.420), kind=kOutput, calls=%fused_computation.52.clone.1 | convolution fusion | flops 671088640 | bytes 4456448 | tf_op jit(solution)/shard_map/while/body/eval_jaxpr/dot_general | solution.py:45
  95.6 0.2 reshape.56
  96.0 1.2 reshape.57
  97.3 0.2 multiply_reduce_fusion.3
  97.7 0.2 dynamic_update_slice.66
  98.0 0.6 copy-done.2
  98.7 5.7 %all-reduce.2 = (f32[32]{0:T(128)S(1)}, f32[32]{0:T(128)S(1)}) all-reduce(f32[32]{0:T(128)S(1)} %get-tuple-element.255, f32[32]{0:T(128)S(1)} %get-tuple-element.253), channel_id=1, replica_groups=mesh['groups'=2,'tm'=4,'chan'=2,'sub'=2] {'chan','sub'}, use_global_device_ids=true, to_apply=%region_12.13 | all-reduce | flops 64 | bytes 512 | tf_op jit(solution)/shard_map/psum | solution.py:123
  104.5 24.9 %all-reduce.6.cloned.1.call-done = (f32[32,1024]{1,0:T(8,128)}, f32[32,1024]{1,0:T(8,128)}) async-done(((f32[32,1024]{1,0:T(8,128)}, f32[32,1024]{1,0:T(8,128)}), (f32[32,1024]{1,0:T(8,128)}, f32[32,1024]{1,0:T(8,128)})) %all-reduce.6.cloned.1.call-update) | async-done | bytes 262160 | tf_op jit(solution)/shard_map/psum | solution.py:123
  129.4 1.5 %rsqrt_multiply_fusion = f32[8,1024]{1,0:T(8,128)} fusion(f32[32,1024]{1,0:T(8,128)} %get-tuple-element.308, s32[]{:T(128)S(6)} %select_n.46, f32[32,1024]{1,0:T(8,128)} %get-tuple-element.309, f32[8]{0:T(128)S(1)} %dynamic_slice.15, f32[8]{0:T(128)S(1)} %multiply_sqrt_fusion), kind=kLoop, calls=%fused_computation.46 | loop fusion | flops 32768 | bytes 98372 | tf_op jit(solution)/shard_map/div | solution.py:64
  (76 shorter events, 3.8 us)
Async XLA Ops:
  6.5 122.9 %all-reduce.6.cloned.1.call-start = ((), (), s32[]{:S(2)}) async-start(), calls=%async_computation | async-start | bytes 524288 | tf_op jit(solution)/shard_map/psum | solution.py:123
  7.4 14.0 %collective-permute-start.2 = (bf16[128,256]{1,0:T(8,128)(2,1)S(1)}, bf16[128,256]{1,0:T(8,128)(2,1)S(1)}, u32[]{:S(2)}, u32[]{:S(2)}) collective-permute-start(bf16[128,256]{1,0:T(8,128)(2,1)S(1)} %slice.100), channel_id=1, source_target_pairs={{0,12},{4,0},{8,4},{12,8},{1,13},{5,1},{9,5},{13,9},{2,14},{6,2},{... | collective-permute-start | bytes 196616 | tf_op jit(solution)/shard_map/ppermute | solution.py:12
  14.9 6.6 %copy-start = (bf16[128,1024]{1,0:T(8,128)(2,1)S(1)}, bf16[128,1024]{1,0:T(8,128)(2,1)}, u32[]{:S(2)}) copy-start(bf16[128,1024]{1,0:T(8,128)(2,1)} %param.5) | copy-start | bytes 786436
  32.2 2.3 %copy-start.1 = (bf16[256,1024]{1,0:T(8,128)(2,1)S(1)}, bf16[256,1024]{1,0:T(8,128)(2,1)}, u32[]{:S(2)}) copy-start(bf16[256,1024]{1,0:T(8,128)(2,1)} %copy.21) | copy-start | bytes 1572868
  34.8 17.0 %collective-permute-start = (bf16[256,1024]{1,0:T(8,128)(2,1)S(1)}, bf16[256,1024]{1,0:T(8,128)(2,1)S(1)}, u32[]{:S(2)}, u32[]{:S(2)}) collective-permute-start(bf16[256,1024]{1,0:T(8,128)(2,1)S(1)} %get-tuple-element.397), channel_id=1, source_target_pairs={{0,4},{4,8},{8,12},{12,0},{1,5},{5,9},{9,13},{13,1},{2,6},{6,10},{... | collective-permute-start | bytes 1572872 | tf_op jit(solution)/shard_map/while/body/eval_jaxpr/ppermute | solution.py:12
  34.8 15.2 %collective-permute-start.1 = (bf16[8,128]{1,0:T(8,128)(2,1)S(1)}, bf16[8,128]{1,0:T(8,128)(2,1)S(1)}, u32[]{:S(2)}, u32[]{:S(2)}) collective-permute-start(bf16[8,128]{1,0:T(8,128)(2,1)S(1)} %get-tuple-element.398), channel_id=1, source_target_pairs={{0,4},{4,8},{8,12},{12,0},{1,5},{5,9},{9,13},{13,1},{2,6},{6,10},{... | collective-permute-start | bytes 6152 | tf_op jit(solution)/shard_map/while/body/eval_jaxpr/ppermute | solution.py:12
  50.4 1.3 copy-start.4
  55.9 0.8 copy-start.5
  56.7 16.1 %collective-permute-start = (bf16[256,1024]{1,0:T(8,128)(2,1)S(1)}, bf16[256,1024]{1,0:T(8,128)(2,1)S(1)}, u32[]{:S(2)}, u32[]{:S(2)}) collective-permute-start(bf16[256,1024]{1,0:T(8,128)(2,1)S(1)} %get-tuple-element.397), channel_id=1, source_target_pairs={{0,4},{4,8},{8,12},{12,0},{1,5},{5,9},{9,13},{13,1},{2,6},{6,10},{... | collective-permute-start | bytes 1572872 | tf_op jit(solution)/shard_map/while/body/eval_jaxpr/ppermute | solution.py:12
  56.8 14.4 %collective-permute-start.1 = (bf16[8,128]{1,0:T(8,128)(2,1)S(1)}, bf16[8,128]{1,0:T(8,128)(2,1)S(1)}, u32[]{:S(2)}, u32[]{:S(2)}) collective-permute-start(bf16[8,128]{1,0:T(8,128)(2,1)S(1)} %get-tuple-element.398), channel_id=1, source_target_pairs={{0,4},{4,8},{8,12},{12,0},{1,5},{5,9},{9,13},{13,1},{2,6},{6,10},{... | collective-permute-start | bytes 6152 | tf_op jit(solution)/shard_map/while/body/eval_jaxpr/ppermute | solution.py:12
  71.5 1.3 copy-start.4
  77.0 0.8 copy-start.5
  77.8 15.2 %collective-permute-start = (bf16[256,1024]{1,0:T(8,128)(2,1)S(1)}, bf16[256,1024]{1,0:T(8,128)(2,1)S(1)}, u32[]{:S(2)}, u32[]{:S(2)}) collective-permute-start(bf16[256,1024]{1,0:T(8,128)(2,1)S(1)} %get-tuple-element.397), channel_id=1, source_target_pairs={{0,4},{4,8},{8,12},{12,0},{1,5},{5,9},{9,13},{13,1},{2,6},{6,10},{... | collective-permute-start | bytes 1572872 | tf_op jit(solution)/shard_map/while/body/eval_jaxpr/ppermute | solution.py:12
  77.8 13.5 %collective-permute-start.1 = (bf16[8,128]{1,0:T(8,128)(2,1)S(1)}, bf16[8,128]{1,0:T(8,128)(2,1)S(1)}, u32[]{:S(2)}, u32[]{:S(2)}) collective-permute-start(bf16[8,128]{1,0:T(8,128)(2,1)S(1)} %get-tuple-element.398), channel_id=1, source_target_pairs={{0,4},{4,8},{8,12},{12,0},{1,5},{5,9},{9,13},{13,1},{2,6},{6,10},{... | collective-permute-start | bytes 6152 | tf_op jit(solution)/shard_map/while/body/eval_jaxpr/ppermute | solution.py:12
  91.7 1.3 copy-start.4
  97.2 0.8 copy-start.5
  98.0 0.7 copy-start.2
  98.0 0.7 copy-start.3
Sparse Core Ops, SparseCore 0:
  98.8 30.5 all-reduce.5
where the time goes:
time: 138 us
  waiting for transfers between devices  67.7 us (49%)
  local copies, waits for them, and re-layouts  21.8 us (16%)
  matrix products  14.9 us (11%)
  between operations  13.6 us (10%)
  other arithmetic  7.98 us (6%)
  blocking collectives  5.67 us (4%)
  starting transfers between devices  5.43 us (4%)
    ppermute x7, waiting for transfers between devices, shifted(): return lax.ppermute(x, axis, [(i, (i + by) % count) for i in range(count)])  42.8 us
    psum x1, waiting for transfers between devices, on_device(): lax.psum(accums, ('chan', 'sub'))  24.9 us
    dot_general x4, matrix products, correlate(): jnp.dot(arranged, frames, preferred_element_type=jnp.float32)  9.65 us
    psum x1, blocking collectives, on_device(): lax.psum(accums, ('chan', 'sub'))  5.67 us
    ppermute x7, starting transfers between devices, shifted(): return lax.ppermute(x, axis, [(i, (i + by) % count) for i in range(count)])  5.43 us
    dot_general x4, matrix products, absorb(): jnp.dot(active, chan_energy, precision=lax.Precision.HIGHEST, preferred_e...  5.3 us
    reshape x4, local copies, waits for them, and re-layouts, correlate(): flattened.reshape(block_rows, lag_blocks, frame_width + lag_step)  4.78 us
    add x3, other arithmetic, window_sums(): running = running + values[:, offset * stride:offset * stride + length]  3.52 us
  transfers between devices with their start and end apart: 8, of which 4 were waited for; matrix products, arithmetic and copies ran while one was open for 10% of the time, Pallas kernels for 0%

commit v1 on v0

v1 whole, which is shorter than its diff:
```python
import functools

import jax
import jax.numpy as jnp
from jax import lax
from jax.experimental import pallas as pl
from jax.experimental.pallas import tpu as pltpu
from jax.sharding import PartitionSpec as P

EPSILON = 1e-06
MESH = pl.DeviceIdType.MESH
LANES = 128
FRAMES = 4
FINE = LANES // FRAMES


def kernel(sizes, x_ref, w_ref, m_ref, o_ref, xb, af, ab, fr, pr, st, tb, rb,
           recv_sem, right_sem, left_sem, out_sem, in_sem):
    tm, chan_n, sub_n = sizes
    cs_n = chan_n * sub_n
    me = lax.axis_index("tm")
    my_chan = lax.axis_index("chan")
    my_sub = lax.axis_index("sub")
    my_cs = my_chan * sub_n + my_sub
    chans, tile = x_ref.shape
    rows, _, span = w_ref.shape
    blocks = tm // cs_n
    coarse = span // FINE
    wide = tile + LANES
    owner = me // blocks
    owner_chan = owner // sub_n
    owner_sub = owner % sub_n

    barrier = pltpu.get_barrier_semaphore()
    count = 0
    for a in range(tm):
        for b in range(chan_n):
            for c in range(sub_n):
                if a or b or c:
                    pl.semaphore_signal(
                        barrier, inc=1,
                        device_id={"tm": lax.rem(me + a, tm),
                                   "chan": lax.rem(my_chan + b, chan_n),
                                   "sub": lax.rem(my_sub + c, sub_n)},
                        device_id_type=MESH)
                    count += 1
    pl.semaphore_wait(barrier, count)

    def relay(src, index, to, sem):
        return pltpu.make_async_remote_copy(
            src_ref=src, dst_ref=xb.at[index], send_sem=sem.at[index],
            recv_sem=recv_sem.at[index], device_id={"tm": to}, device_id_type=MESH)

    @pl.when(me < tm - 1)
    def _():
        relay(x_ref, me, me + 1, right_sem).start()

    @pl.when(me > 0)
    def _():
        relay(x_ref, me, me - 1, left_sem).start()

    xb[me] = x_ref[...]

    mask = m_ref[...].astype(jnp.float32)
    for k in range(rows):
        wave = jnp.transpose(w_ref[k].astype(jnp.float32)) * mask[k : k + 1, :]
        tb[k : k + 1, :] = jnp.sum(wave * wave, axis=0, keepdims=True)
        for g in range(coarse):
            af[g, pl.ds(k, FINE, stride=rows), :] = wave[g * FINE : (g + 1) * FINE, :]
    for g in range(coarse):
        ab[:, g * chans : (g + 1) * chans] = af[g].astype(jnp.bfloat16)
    mask_bf = mask.astype(jnp.bfloat16)
    mask_two = jnp.concatenate([mask_bf, mask_bf], 1)
    local_slot = (me % blocks) * cs_n + my_cs

    def result_copy(t):
        return pltpu.make_async_remote_copy(
            src_ref=st.at[t], dst_ref=rb.at[local_slot], send_sem=out_sem.at[t],
            recv_sem=in_sem.at[local_slot],
            device_id={"tm": t, "chan": owner_chan, "sub": owner_sub}, device_id_type=MESH)

    def process(t):
        after = lax.rem(t + 1, tm)
        ext = jnp.concatenate([xb[t], xb[after, :, : span + LANES]], 1)
        for f in range(FRAMES):
            moved = ext[:, f * FINE : f * FINE + tile + span]
            for h in range(span // LANES):
                g = h * FRAMES + f
                fr[g * chans : (g + 1) * chans, :] = moved[:, h * LANES : h * LANES + wide]
        pr[...] = jnp.dot(ab[...], fr[...], preferred_element_type=jnp.float32)
        corr = pr[0:rows, :tile]
        for b in range(1, FINE):
            corr = corr + pltpu.roll(pr[b * rows : (b + 1) * rows, :], wide - b, 1)[:, :tile]
        x32 = ext[:, : tile + span].astype(jnp.float32)
        square = x32 * x32
        high = square.astype(jnp.bfloat16)
        low = (square - high.astype(jnp.float32)).astype(jnp.bfloat16)
        power = jnp.dot(mask_two, jnp.concatenate([high, low], 0),
                        preferred_element_type=jnp.float32)
        by = 1
        while by < span:
            power = power + pltpu.roll(power, tile + span - by, 1)
            by *= 2
        power = power[:, :tile]
        own = jnp.logical_and(t == me, my_cs == owner)

        @pl.when(own)
        def _():
            rb[local_slot, 0:rows, 0:tile] = corr
            rb[local_slot, rows : 2 * rows, 0:tile] = power
            rb[local_slot, 0:rows, tile:] = tb[...]
            rb[local_slot, rows : 2 * rows, tile:] = mask

        @pl.when(jnp.logical_not(own))
        def _():
            st[t, 0:rows, 0:tile] = corr
            st[t, rows : 2 * rows, 0:tile] = power
            st[t, 0:rows, tile:] = tb[...]
            st[t, rows : 2 * rows, tile:] = mask
            result_copy(t).start()

    def step(u, carry):
        i = u // 2
        right_side = u % 2 == 0
        last = u == 2 * (tm - 1)
        from_left = me - 1 - i
        from_right = me + 1 + i
        first = jnp.logical_and(right_side, jnp.logical_not(last))

        @pl.when(jnp.logical_and(first, from_left >= 0))
        def _():
            relay(x_ref, from_left, me, right_sem).wait_recv()

            @pl.when(me < tm - 1)
            def _():
                relay(xb.at[from_left], from_left, me + 1, right_sem).start()

        @pl.when(jnp.logical_and(first, from_right <= tm - 1))
        def _():
            relay(x_ref, from_right, me, left_sem).wait_recv()

            @pl.when(me > 0)
            def _():
                relay(xb.at[from_right], from_right, me - 1, left_sem).start()

        t = jnp.where(last, tm - 1, jnp.where(right_side, me + i, from_left))
        valid = jnp.logical_or(
            last, jnp.logical_or(jnp.logical_and(right_side, from_right <= tm - 1),
                                 jnp.logical_and(jnp.logical_not(right_side), from_left >= 0)))

        @pl.when(valid)
        def _():
            process(t)

        return carry

    lax.fori_loop(0, 2 * (tm - 1) + 1, step, 0)

    def finish(t, carry):
        @pl.when(jnp.logical_and(me < tm - 1, t <= me))
        def _():
            relay(x_ref, t, me, right_sem).wait_send()

        @pl.when(jnp.logical_and(me > 0, t >= me))
        def _():
            relay(x_ref, t, me, left_sem).wait_send()

        @pl.when(jnp.logical_not(jnp.logical_and(t == me, my_cs == owner)))
        def _():
            result_copy(t).wait_send()

        return carry

    lax.fori_loop(0, tm, finish, 0)

    for q in range(blocks):
        for c in range(cs_n):
            slot = q * cs_n + c
            mine = jnp.logical_and(my_cs == owner, slot == local_slot)

            @pl.when(jnp.logical_not(mine))
            def _():
                pltpu.make_async_remote_copy(
                    src_ref=st.at[0], dst_ref=rb.at[slot], send_sem=out_sem.at[0],
                    recv_sem=in_sem.at[slot],
                    device_id={"tm": me}, device_id_type=MESH).wait_recv()

    for q in range(blocks):
        total = rb[q * cs_n]
        for c in range(1, cs_n):
            total = total + rb[q * cs_n + c]
        te = jnp.sum(total[0:rows, tile:], axis=1, keepdims=True)
        active = jnp.sum(total[rows : 2 * rows, tile:], axis=1, keepdims=True)
        factor = jnp.sqrt(span * active)
        o_ref[q * rows : (q + 1) * rows, :] = (
            total[0:rows, :tile] * factor
            / jnp.sqrt(total[rows : 2 * rows, :tile] * te + EPSILON))


def solution(mesh):
    tm, chan_n, sub_n = (mesh.shape[a] for a in ("tm", "chan", "sub"))
    cs_n = chan_n * sub_n
    blocks = tm // cs_n

    def on_device(traces, templates, channel_mask):
        chans, tile = traces.shape
        rows, _, span = templates.shape
        coarse = span // FINE
        wide = tile + LANES
        vmem = pl.BlockSpec(memory_space=pltpu.VMEM)
        return pl.pallas_call(
            functools.partial(kernel, (tm, chan_n, sub_n)),
            out_shape=jax.ShapeDtypeStruct((blocks * rows, tile), jnp.float32),
            in_specs=[vmem] * 3,
            out_specs=vmem,
            scratch_shapes=[
                pltpu.VMEM((tm, chans, tile), jnp.bfloat16),
                pltpu.VMEM((coarse, FINE * rows, chans), jnp.float32),
                pltpu.VMEM((FINE * rows, coarse * chans), jnp.bfloat16),
                pltpu.VMEM((coarse * chans, wide), jnp.bfloat16),
                pltpu.VMEM((FINE * rows, wide), jnp.float32),
                pltpu.VMEM((tm, 2 * rows, wide), jnp.float32),
                pltpu.VMEM((rows, chans), jnp.float32),
                pltpu.VMEM((blocks * cs_n, 2 * rows, wide), jnp.float32),
                pltpu.SemaphoreType.DMA((tm,)),
                pltpu.SemaphoreType.DMA((tm,)),
                pltpu.SemaphoreType.DMA((tm,)),
                pltpu.SemaphoreType.DMA((tm,)),
                pltpu.SemaphoreType.DMA((blocks * cs_n,)),
            ],
            compiler_params=pltpu.CompilerParams(collective_id=0, has_side_effects=True),
        )(traces, templates, channel_mask)

    placed = (
        P(("chan", "sub"), ("groups", "tm")),
        P("tm", ("chan", "sub"), None),
        P("tm", ("chan", "sub")),
    )
    return jax.shard_map(
        on_device,
        mesh=mesh,
        in_specs=placed,
        out_specs=P(("chan", "sub"), ("groups", "tm")),
        check_vma=False,
    )
```

time: 138 us -> 38.2 us (0.28)
  waiting for transfers between devices: 67.7 us -> 0 us
  Pallas kernels: 0 us -> 36.6 us
  local copies, waits for them, and re-layouts: 21.8 us -> 1.38 us
  matrix products: 14.9 us -> 0 us
  between operations: 13.6 us -> 0.01 us
  other arithmetic: 7.98 us -> 0 us
  blocking collectives: 5.67 us -> 0 us
  starting transfers between devices: 5.43 us -> 0 us
    ppermute x7 -> x0, waiting for transfers between devices: 42.8 us -> none  [shifted(): return lax.ppermute(x, axis, [(i, (i + by) % count) for i in range(count)])]
    pallas_call x0 -> x1, Pallas kernels: none -> 36.6 us  [on_device(): pl.pallas_call(functools.partial(kernel, (tm, chan_n, sub_n)), out_shape=...]
    psum x1 -> x0, waiting for transfers between devices: 24.9 us -> none  [on_device(): lax.psum(accums, ('chan', 'sub'))]
    dot_general x8 -> x0, matrix products: 14.9 us -> none  [the longest x4 9.65 us: correlate(): jnp.dot(arranged, frames, preferred_element_type=jnp.float32)]
    reshape x9 -> x0, local copies, waits for them, and re-layouts: 7.37 us -> none  [the longest x4 4.78 us: correlate(): flattened.reshape(block_rows, lag_blocks, frame_width + lag_step)]
    psum x1 -> x0, blocking collectives: 5.67 us -> none  [on_device(): lax.psum(accums, ('chan', 'sub'))]
    ppermute x7 -> x0, starting transfers between devices: 5.43 us -> none  [shifted(): return lax.ppermute(x, axis, [(i, (i + by) % count) for i in range(count)])]
    add x3 -> x0, other arithmetic: 3.52 us -> none  [window_sums(): running = running + values[:, offset * stride:offset * stride + length]]
  transfers between devices with their start and end apart: 8 -> 0, of which waited for: 4 -> 0; matrix products, arithmetic and copies ran while one was open for 10% -> 0% of each run, Pallas kernels for 0% -> 0%
where the time goes in v1:
time: 38.2 us; the launch traced here: 38 us
  Pallas kernels  36.6 us (96%)
  local copies, waits for them, and re-layouts  1.38 us (4%)
    pallas_call x1, Pallas kernels, on_device(): pl.pallas_call(functools.partial(kernel, (tm, chan_n, sub_n)), out_shape=...  36.6 us
    unnamed x1, local copies, waits for them, and re-layouts  1.38 us

profile of v1, /device:TPU:0, one launch (start us, length us, event | category | flops | bytes accessed | tf_op | source)
XLA Modules:
  0.0 38.0 jit_solution(3694858054792887477)
XLA Ops:
  0.0 36.6 %shard_map.37 = f32[8,1024]{1,0:T(8,128)} custom-call(bf16[128,1024]{1,0:T(8,128)(2,1)} %x_ref.1, bf16[8,128,256]{2,1,0:T(8,128)(2,1)} %w_ref.1, s32[8,128]{1,0:T(8,128)} %m_ref.1), custom_call_target="tpu_custom_call" | custom-call | tf_op jit(solution)/shard_map/pallas_call | solution.py:211
  36.6 1.4 %copy.5 = f32[8,1024]{1,0:T(8,128)} copy(f32[8,1024]{1,0:T(8,128)} %shard_map.37) | data formatting | bytes 65536

commit v2 on v1

v2 whole, which is shorter than its diff:
```python
import functools

import jax
import jax.numpy as jnp
from jax import lax
from jax.experimental import pallas as pl
from jax.experimental.pallas import tpu as pltpu
from jax.sharding import PartitionSpec as P

EPSILON = 1e-06
MESH = pl.DeviceIdType.MESH
LANES = 128
FRAMES = 4
FINE = LANES // FRAMES
PIECES = 2


def kernel(sizes, x_ref, w_ref, m_ref, o_ref, xb, af, ab, fr, pr, st, tb, rb, fin, ob,
           recv_sem, right_sem, left_sem, out_sem, in_sem, score_sem, done_sem):
    tm, chan_n, sub_n = sizes
    cs_n = chan_n * sub_n
    me = lax.axis_index("tm")
    my_chan = lax.axis_index("chan")
    my_sub = lax.axis_index("sub")
    my_cs = my_chan * sub_n + my_sub
    chans, tile = x_ref.shape
    rows, _, span = w_ref.shape
    blocks = tm // cs_n
    coarse = span // FINE
    wide = tile + LANES
    part = chans // PIECES
    owner = me // blocks

    barrier = pltpu.get_barrier_semaphore()

    @pl.when(me < tm - 1)
    def _():
        pl.semaphore_signal(barrier, inc=1, device_id={"tm": me + 1}, device_id_type=MESH)

    @pl.when(me > 0)
    def _():
        pl.semaphore_signal(barrier, inc=1, device_id={"tm": me - 1}, device_id_type=MESH)

    for b in range(chan_n):
        for c in range(sub_n):
            if b or c:
                pl.semaphore_signal(
                    barrier, inc=1,
                    device_id={"chan": lax.rem(my_chan + b, chan_n),
                               "sub": lax.rem(my_sub + c, sub_n)},
                    device_id_type=MESH)

    xb[me] = x_ref[...]
    mask = m_ref[...].astype(jnp.float32)
    for k in range(rows):
        wave = jnp.transpose(w_ref[k].astype(jnp.float32)) * mask[k : k + 1, :]
        tb[k : k + 1, :] = jnp.sum(wave * wave, axis=0, keepdims=True)
        for g in range(coarse):
            af[g, pl.ds(k, FINE, stride=rows), :] = wave[g * FINE : (g + 1) * FINE, :]
    for g in range(coarse):
        ab[:, g * chans : (g + 1) * chans] = af[g].astype(jnp.bfloat16)
    mask_bf = mask.astype(jnp.bfloat16)
    mask_two = jnp.concatenate([mask_bf, mask_bf], 1)

    at_end = jnp.logical_or(me == 0, me == tm - 1)
    pl.semaphore_wait(barrier, cs_n - 1 + jnp.where(at_end, 1, 2))

    def relay(src, index, p, to, sem):
        rows_of = pl.ds(p * part, part)
        return pltpu.make_async_remote_copy(
            src_ref=src.at[rows_of], dst_ref=xb.at[index, rows_of], send_sem=sem.at[index, p],
            recv_sem=recv_sem.at[index, p], device_id={"tm": to}, device_id_type=MESH)

    for p in range(PIECES):
        @pl.when(me < tm - 1)
        def _():
            relay(x_ref, me, p, me + 1, right_sem).start()

        @pl.when(me > 0)
        def _():
            relay(x_ref, me, p, me - 1, left_sem).start()

    def sum_copy(t):
        at = t % cs_n
        slot = (t // cs_n) * cs_n + my_cs
        return pltpu.make_async_remote_copy(
            src_ref=st.at[t], dst_ref=rb.at[slot], send_sem=out_sem.at[t],
            recv_sem=in_sem.at[slot],
            device_id={"chan": at // sub_n, "sub": at % sub_n}, device_id_type=MESH)

    def score_copy(q):
        return pltpu.make_async_remote_copy(
            src_ref=fin.at[q], dst_ref=ob.at[me % blocks], send_sem=score_sem.at[q],
            recv_sem=done_sem.at[me % blocks],
            device_id={"tm": q * cs_n + my_cs, "chan": owner // sub_n, "sub": owner % sub_n},
            device_id_type=MESH)

    def process(t):
        after = lax.rem(t + 1, tm)
        ext = jnp.concatenate([xb[t], xb[after, :, : span + LANES]], 1)
        for f in range(FRAMES):
            moved = ext[:, f * FINE : f * FINE + tile + span]
            for h in range(span // LANES):
                g = h * FRAMES + f
                fr[g * chans : (g + 1) * chans, :] = moved[:, h * LANES : h * LANES + wide]
        pr[...] = jnp.dot(ab[...], fr[...], preferred_element_type=jnp.float32)
        corr = pr[0:rows, :tile]
        for b in range(1, FINE):
            corr = corr + pltpu.roll(pr[b * rows : (b + 1) * rows, :], wide - b, 1)[:, :tile]
        x32 = ext[:, : tile + span].astype(jnp.float32)
        square = x32 * x32
        high = square.astype(jnp.bfloat16)
        low = (square - high.astype(jnp.float32)).astype(jnp.bfloat16)
        power = jnp.dot(mask_two, jnp.concatenate([high, low], 0),
                        preferred_element_type=jnp.float32)
        by = 1
        while by < span:
            power = power + pltpu.roll(power, tile + span - by, 1)
            by *= 2
        power = power[:, :tile]

        def put(ref, index):
            ref[index, 0:rows, 0:tile] = corr
            ref[index, rows : 2 * rows, 0:tile] = power
            ref[index, 0:rows, tile:] = tb[...]
            ref[index, rows : 2 * rows, tile:] = mask

        own = t % cs_n == my_cs

        @pl.when(own)
        def _():
            put(rb, (t // cs_n) * cs_n + my_cs)

        @pl.when(jnp.logical_not(own))
        def _():
            put(st, t)
            sum_copy(t).start()

    def step(u, carry):
        i = u // 2
        right_side = u % 2 == 0
        last = u == 2 * (tm - 1)
        from_left = me - 1 - i
        from_right = me + 1 + i
        first = jnp.logical_and(right_side, jnp.logical_not(last))

        for p in range(PIECES):
            @pl.when(jnp.logical_and(first, from_left >= 0))
            def _():
                relay(x_ref, from_left, p, me, right_sem).wait_recv()

                @pl.when(me < tm - 1)
                def _():
                    relay(xb.at[from_left], from_left, p, me + 1, right_sem).start()

            @pl.when(jnp.logical_and(first, from_right <= tm - 1))
            def _():
                relay(x_ref, from_right, p, me, left_sem).wait_recv()

                @pl.when(me > 0)
                def _():
                    relay(xb.at[from_right], from_right, p, me - 1, left_sem).start()

        t = jnp.where(last, tm - 1, jnp.where(right_side, me + i, from_left))
        valid = jnp.logical_or(
            last, jnp.logical_or(jnp.logical_and(right_side, from_right <= tm - 1),
                                 jnp.logical_and(jnp.logical_not(right_side), from_left >= 0)))

        @pl.when(valid)
        def _():
            process(t)

        return carry

    lax.fori_loop(0, 2 * (tm - 1) + 1, step, 0)

    for q in range(blocks):
        t = q * cs_n + my_cs
        for c in range(cs_n):
            @pl.when(my_cs != c)
            def _():
                pltpu.make_async_remote_copy(
                    src_ref=st.at[0], dst_ref=rb.at[q * cs_n + c], send_sem=out_sem.at[0],
                    recv_sem=in_sem.at[q * cs_n + c],
                    device_id={"tm": me}, device_id_type=MESH).wait_recv()
        total = rb[q * cs_n]
        for c in range(1, cs_n):
            total = total + rb[q * cs_n + c]
        te = jnp.sum(total[0:rows, tile:], axis=1, keepdims=True)
        active = jnp.sum(total[rows : 2 * rows, tile:], axis=1, keepdims=True)
        factor = jnp.sqrt(span * active)
        scores = (total[0:rows, :tile] * factor
                  / jnp.sqrt(total[rows : 2 * rows, :tile] * te + EPSILON))
        here = jnp.logical_and(t == me, my_cs == owner)

        @pl.when(here)
        def _():
            ob[me % blocks] = scores

        @pl.when(jnp.logical_not(here))
        def _():
            fin[q] = scores
            score_copy(q).start()

    def finish(t, carry):
        for p in range(PIECES):
            @pl.when(jnp.logical_and(me < tm - 1, t <= me))
            def _():
                relay(x_ref, t, p, me, right_sem).wait_send()

            @pl.when(jnp.logical_and(me > 0, t >= me))
            def _():
                relay(x_ref, t, p, me, left_sem).wait_send()

        @pl.when(t % cs_n != my_cs)
        def _():
            sum_copy(t).wait_send()

        return carry

    lax.fori_loop(0, tm, finish, 0)

    for q in range(blocks):
        here = jnp.logical_and(q * cs_n + my_cs == me, my_cs == owner)

        @pl.when(jnp.logical_not(here))
        def _():
            score_copy(q).wait_send()

    for q in range(blocks):
        here = jnp.logical_and(my_cs * blocks + q == me, me % cs_n == my_cs)

        @pl.when(jnp.logical_not(here))
        def _():
            pltpu.make_async_remote_copy(
                src_ref=fin.at[0], dst_ref=ob.at[q], send_sem=score_sem.at[0],
                recv_sem=done_sem.at[q],
                device_id={"tm": me}, device_id_type=MESH).wait_recv()
        o_ref[q * rows : (q + 1) * rows, :] = ob[q]


def solution(mesh):
    tm, chan_n, sub_n = (mesh.shape[a] for a in ("tm", "chan", "sub"))
    cs_n = chan_n * sub_n
    blocks = tm // cs_n

    def on_device(traces, templates, channel_mask):
        chans, tile = traces.shape
        rows, _, span = templates.shape
        coarse = span // FINE
        wide = tile + LANES
        vmem = pl.BlockSpec(memory_space=pltpu.VMEM)
        return pl.pallas_call(
            functools.partial(kernel, (tm, chan_n, sub_n)),
            out_shape=jax.ShapeDtypeStruct((blocks * rows, tile), jnp.float32),
            in_specs=[vmem] * 3,
            out_specs=vmem,
            scratch_shapes=[
                pltpu.VMEM((tm, chans, tile), jnp.bfloat16),
                pltpu.VMEM((coarse, FINE * rows, chans), jnp.float32),
                pltpu.VMEM((FINE * rows, coarse * chans), jnp.bfloat16),
                pltpu.VMEM((coarse * chans, wide), jnp.bfloat16),
                pltpu.VMEM((FINE * rows, wide), jnp.float32),
                pltpu.VMEM((tm, 2 * rows, wide), jnp.float32),
                pltpu.VMEM((rows, chans), jnp.float32),
                pltpu.VMEM((blocks * cs_n, 2 * rows, wide), jnp.float32),
                pltpu.VMEM((blocks, rows, tile), jnp.float32),
                pltpu.VMEM((blocks, rows, tile), jnp.float32),
                pltpu.SemaphoreType.DMA((tm, PIECES)),
                pltpu.SemaphoreType.DMA((tm, PIECES)),
                pltpu.SemaphoreType.DMA((tm, PIECES)),
                pltpu.SemaphoreType.DMA((tm,)),
                pltpu.SemaphoreType.DMA((blocks * cs_n,)),
                pltpu.SemaphoreType.DMA((blocks,)),
                pltpu.SemaphoreType.DMA((blocks,)),
            ],
            compiler_params=pltpu.CompilerParams(collective_id=0, has_side_effects=True),
        )(traces, templates, channel_mask)

    placed = (
        P(("chan", "sub"), ("groups", "tm")),
        P("tm", ("chan", "sub"), None),
        P("tm", ("chan", "sub")),
    )
    return jax.shard_map(
        on_device,
        mesh=mesh,
        in_specs=placed,
        out_specs=P(("chan", "sub"), ("groups", "tm")),
        check_vma=False,
    )
```

time: 38.2 us -> 34 us (0.89)
  the two profiles are of different devices: /device:TPU:0 before, /device:TPU:3 now
where the time goes in v2:
time: 34 us; the launch traced here: 33.8 us
  Pallas kernels  32.4 us (95%)
  local copies, waits for them, and re-layouts  1.38 us (4%)
    pallas_call x1, Pallas kernels, on_device(): pl.pallas_call(functools.partial(kernel, (tm, chan_n, sub_n)), out_shape=...  32.4 us
    unnamed x1, local copies, waits for them, and re-layouts  1.38 us

profile of v2, /device:TPU:3, one launch (start us, length us, event | category | flops | bytes accessed | tf_op | source)
XLA Modules:
  0.0 33.8 jit_solution(6877603649016163828)
XLA Ops:
  0.0 32.4 %shard_map.37 = f32[8,1024]{1,0:T(8,128)} custom-call(bf16[128,1024]{1,0:T(8,128)(2,1)} %x_ref.1, bf16[8,128,256]{2,1,0:T(8,128)(2,1)} %w_ref.1, s32[8,128]{1,0:T(8,128)} %m_ref.1), custom_call_target="tpu_custom_call" | custom-call | tf_op jit(solution)/shard_map/pallas_call | solution.py:253
  32.4 1.4 %copy.5 = f32[8,1024]{1,0:T(8,128)} copy(f32[8,1024]{1,0:T(8,128)} %shard_map.37) | data formatting | bytes 65536

commit v3 on v2

v3 whole, which is shorter than its diff:
```python
import functools

import jax
import jax.numpy as jnp
from jax import lax
from jax.experimental import pallas as pl
from jax.experimental.pallas import tpu as pltpu
from jax.sharding import PartitionSpec as P

EPSILON = 1e-06
MESH = pl.DeviceIdType.MESH
LANES = 128
FRAMES = 4
FINE = LANES // FRAMES
PIECES = 2


def kernel(sizes, x_ref, w_ref, m_ref, o_ref, xb, af, ab, fr, pr, st, tb, rb, fin, ob, wx, mx,
           recv_sem, right_sem, left_sem, out_sem, in_sem, score_sem, done_sem,
           wave_out, wave_in, swap_out, mask_out, mask_in):
    group_n, tm, chan_n, sub_n = sizes
    group = lax.axis_index("groups")
    cs_n = chan_n * sub_n
    me = lax.axis_index("tm")
    my_chan = lax.axis_index("chan")
    my_sub = lax.axis_index("sub")
    my_cs = my_chan * sub_n + my_sub
    chans, tile = x_ref.shape
    rows, _, span = w_ref.shape
    blocks = tm // cs_n
    coarse = span // FINE
    wide = tile + LANES
    part = chans // PIECES
    owner = me // blocks
    share = rows // group_n
    my_at = my_sub * chan_n + my_chan
    is_end = jnp.logical_or(me == 0, me == tm - 1)
    is_helper = jnp.logical_or(me == 1, me == tm - 2)
    inner = jnp.where(me == 0, 1, tm - 2)
    extra_block = jnp.where(me == 1, 0, tm - 1)
    extra_tile = jnp.where(me == 1, tm - 1, 0)

    def skipped(t):
        return jnp.logical_or(jnp.logical_and(me == 0, t == tm - 1),
                              jnp.logical_and(me == tm - 1, t == 0))

    def place(t):
        at = t % cs_n
        return at % chan_n, at // chan_n

    barrier = pltpu.get_barrier_semaphore()

    @pl.when(me < tm - 1)
    def _():
        pl.semaphore_signal(barrier, inc=1, device_id={"tm": me + 1}, device_id_type=MESH)

    @pl.when(me > 0)
    def _():
        pl.semaphore_signal(barrier, inc=1, device_id={"tm": me - 1}, device_id_type=MESH)

    for b in range(chan_n):
        for c in range(sub_n):
            if b or c:
                pl.semaphore_signal(
                    barrier, inc=1,
                    device_id={"chan": lax.rem(my_chan + b, chan_n),
                               "sub": lax.rem(my_sub + c, sub_n)},
                    device_id_type=MESH)

    for d in range(1, group_n):
        pl.semaphore_signal(barrier, inc=1,
                            device_id={"groups": lax.rem(group + d, group_n)},
                            device_id_type=MESH)

    xb[me] = x_ref[...]

    def prepare(waves, used):
        mask = used[...].astype(jnp.float32)
        for k in range(rows):
            wave = jnp.transpose(waves[k].astype(jnp.float32)) * mask[k : k + 1, :]
            tb[k : k + 1, :] = jnp.sum(wave * wave, axis=0, keepdims=True)
            for g in range(coarse):
                af[g, pl.ds(k, FINE, stride=rows), :] = wave[g * FINE : (g + 1) * FINE, :]
        for g in range(coarse):
            ab[:, g * chans : (g + 1) * chans] = af[g].astype(jnp.bfloat16)

    prepare(w_ref, m_ref)

    pl.semaphore_wait(barrier, cs_n - 1 + group_n - 1 + jnp.where(is_end, 1, 2))

    def relay(method, src, index, p, to, sem, when):
        rightward = sem is right_sem
        far = jnp.logical_and(to == tm - 1, index == 0) if rightward else jnp.logical_and(
            to == 0, index == tm - 1)
        rows_of = pl.ds(p * part, part)
        for short in (False, True):
            columns = pl.ds(0, span if short else tile)

            @pl.when(jnp.logical_and(when, far if short else jnp.logical_not(far)))
            def _():
                getattr(pltpu.make_async_remote_copy(
                    src_ref=src.at[rows_of, columns], dst_ref=xb.at[index, rows_of, columns],
                    send_sem=sem.at[index, p], recv_sem=recv_sem.at[index, p],
                    device_id={"tm": to}, device_id_type=MESH), method)()

    for p in range(PIECES):
        relay("start", x_ref, me, p, me + 1, right_sem, me < tm - 1)
        relay("start", x_ref, me, p, me - 1, left_sem, me > 0)

    def wave_copy(k):
        return pltpu.make_async_remote_copy(
            src_ref=w_ref.at[k], dst_ref=wx.at[k], send_sem=wave_out.at[k],
            recv_sem=wave_in.at[k], device_id={"tm": inner}, device_id_type=MESH)

    def swap_copy(k, d):
        return pltpu.make_async_remote_copy(
            src_ref=wx.at[k], dst_ref=wx.at[k], send_sem=swap_out.at[d - 1, k],
            recv_sem=wave_in.at[k], device_id={"groups": lax.rem(group + d, group_n)},
            device_id_type=MESH)

    def mask_copy():
        return pltpu.make_async_remote_copy(
            src_ref=m_ref, dst_ref=mx, send_sem=mask_out, recv_sem=mask_in,
            device_id={"tm": inner}, device_id_type=MESH)

    @pl.when(is_end)
    def _():
        mask_copy().start()
        for k in range(share):
            wave_copy(group * share + k).start()

    def sum_copy(t):
        slot = (t // cs_n) * cs_n + my_cs
        to_chan, to_sub = place(t)
        return pltpu.make_async_remote_copy(
            src_ref=st.at[t], dst_ref=rb.at[slot], send_sem=out_sem.at[t],
            recv_sem=in_sem.at[slot],
            device_id={"chan": to_chan, "sub": to_sub}, device_id_type=MESH)

    def extra_copy():
        slot = blocks * cs_n + my_cs
        to_chan, to_sub = place(extra_tile)
        return pltpu.make_async_remote_copy(
            src_ref=st.at[tm], dst_ref=rb.at[slot], send_sem=out_sem.at[tm],
            recv_sem=in_sem.at[slot],
            device_id={"chan": to_chan, "sub": to_sub}, device_id_type=MESH)

    def score_copy(q):
        return pltpu.make_async_remote_copy(
            src_ref=fin.at[q], dst_ref=ob.at[me % blocks], send_sem=score_sem.at[q],
            recv_sem=done_sem.at[me % blocks],
            device_id={"tm": q * cs_n + my_at, "chan": owner // sub_n, "sub": owner % sub_n},
            device_id_type=MESH)

    def extra_score_copy():
        to = extra_block // blocks
        return pltpu.make_async_remote_copy(
            src_ref=fin.at[blocks], dst_ref=ob.at[extra_block % blocks],
            send_sem=score_sem.at[blocks], recv_sem=done_sem.at[extra_block % blocks],
            device_id={"tm": extra_tile, "chan": to // sub_n, "sub": to % sub_n},
            device_id_type=MESH)

    def process(t, used, extra):
        mask = used[...].astype(jnp.float32)
        mask_bf = mask.astype(jnp.bfloat16)
        mask_two = jnp.concatenate([mask_bf, mask_bf], 1)
        after = lax.rem(t + 1, tm)
        ext = jnp.concatenate(
            [xb[t], xb[after, :, :span], jnp.zeros((chans, LANES), jnp.bfloat16)], 1)
        for f in range(FRAMES):
            moved = ext[:, f * FINE : f * FINE + tile + span]
            for h in range(span // LANES):
                g = h * FRAMES + f
                fr[g * chans : (g + 1) * chans, :] = moved[:, h * LANES : h * LANES + wide]
        pr[...] = jnp.dot(ab[...], fr[...], preferred_element_type=jnp.float32)
        corr = pr[0:rows, :tile]
        for b in range(1, FINE):
            corr = corr + pltpu.roll(pr[b * rows : (b + 1) * rows, :], wide - b, 1)[:, :tile]
        x32 = ext[:, : tile + span].astype(jnp.float32)
        square = x32 * x32
        high = square.astype(jnp.bfloat16)
        low = (square - high.astype(jnp.float32)).astype(jnp.bfloat16)
        power = jnp.dot(mask_two, jnp.concatenate([high, low], 0),
                        preferred_element_type=jnp.float32)
        by = 1
        while by < span:
            power = power + pltpu.roll(power, tile + span - by, 1)
            by *= 2
        power = power[:, :tile]

        def put(ref, index):
            ref[index, 0:rows, 0:tile] = corr
            ref[index, rows : 2 * rows, 0:tile] = power
            ref[index, 0:rows, tile:] = tb[...]
            ref[index, rows : 2 * rows, tile:] = mask

        own = t % cs_n == my_at

        @pl.when(own)
        def _():
            put(rb, (blocks if extra else t // cs_n) * cs_n + my_cs)

        @pl.when(jnp.logical_not(own))
        def _():
            put(st, tm if extra else t)
            (extra_copy() if extra else sum_copy(t)).start()

    def step(u, carry):
        i = u // 2
        right_side = u % 2 == 0
        last = u == 2 * (tm - 1)
        from_left = me - 1 - i
        from_right = me + 1 + i
        first = jnp.logical_and(right_side, jnp.logical_not(last))

        left_ok = jnp.logical_and(first, from_left >= 0)
        right_ok = jnp.logical_and(first, from_right <= tm - 1)
        for p in range(PIECES):
            relay("wait_recv", x_ref, from_left, p, me, right_sem, left_ok)
            relay("start", xb.at[from_left], from_left, p, me + 1, right_sem,
                  jnp.logical_and(left_ok, me < tm - 1))
            relay("wait_recv", x_ref, from_right, p, me, left_sem, right_ok)
            relay("start", xb.at[from_right], from_right, p, me - 1, left_sem,
                  jnp.logical_and(right_ok, me > 0))

        @pl.when(jnp.logical_and(jnp.logical_and(first, i == tm - 3), is_helper))
        def _():
            for r in range(share):
                k = group * share + r
                wave_copy(k).wait_recv()
                for d in range(1, group_n):
                    swap_copy(k, d).start()

        t = jnp.where(last, tm - 1, jnp.where(right_side, me + i, from_left))
        valid = jnp.logical_or(
            last, jnp.logical_or(jnp.logical_and(right_side, from_right <= tm - 1),
                                 jnp.logical_and(jnp.logical_not(right_side), from_left >= 0)))

        @pl.when(jnp.logical_and(valid, jnp.logical_not(skipped(t))))
        def _():
            process(t, m_ref, False)

        return carry

    lax.fori_loop(0, 2 * (tm - 1) + 1, step, 0)

    @pl.when(is_helper)
    def _():
        mask_copy().wait_recv()
        for r in range(share, rows):
            wave_copy(lax.rem(group * share + r, rows)).wait_recv()
        prepare(wx, mx)
        process(extra_tile, mx, True)

    def reduced(q):
        for c in range(cs_n):
            @pl.when(my_cs != c)
            def _():
                pltpu.make_async_remote_copy(
                    src_ref=st.at[0], dst_ref=rb.at[q * cs_n + c], send_sem=out_sem.at[0],
                    recv_sem=in_sem.at[q * cs_n + c],
                    device_id={"tm": me}, device_id_type=MESH).wait_recv()
        total = rb[q * cs_n]
        for c in range(1, cs_n):
            total = total + rb[q * cs_n + c]
        te = jnp.sum(total[0:rows, tile:], axis=1, keepdims=True)
        active = jnp.sum(total[rows : 2 * rows, tile:], axis=1, keepdims=True)
        factor = jnp.sqrt(span * active)
        return (total[0:rows, :tile] * factor
                / jnp.sqrt(total[rows : 2 * rows, :tile] * te + EPSILON))

    def at_home(q):
        return jnp.logical_and(q * cs_n + my_at == me, my_cs == owner)

    for q in range(blocks):
        @pl.when(jnp.logical_not(skipped(q * cs_n + my_at)))
        def _():
            scores = reduced(q)

            @pl.when(at_home(q))
            def _():
                ob[me % blocks] = scores

            @pl.when(jnp.logical_not(at_home(q)))
            def _():
                fin[q] = scores
                score_copy(q).start()

    extra_here = jnp.logical_and(is_helper, extra_tile % cs_n == my_at)

    @pl.when(extra_here)
    def _():
        fin[blocks] = reduced(blocks)
        extra_score_copy().start()

    def finish(t, carry):
        for p in range(PIECES):
            relay("wait_send", x_ref, t, p, me + 1, right_sem,
                  jnp.logical_and(me < tm - 1, t <= me))
            relay("wait_send", x_ref, t, p, me - 1, left_sem, jnp.logical_and(me > 0, t >= me))

        @pl.when(jnp.logical_and(t % cs_n != my_at, jnp.logical_not(skipped(t))))
        def _():
            sum_copy(t).wait_send()

        return carry

    lax.fori_loop(0, tm, finish, 0)

    @pl.when(is_end)
    def _():
        mask_copy().wait_send()
        for k in range(share):
            wave_copy(group * share + k).wait_send()

    @pl.when(is_helper)
    def _():
        for r in range(share):
            for d in range(1, group_n):
                swap_copy(group * share + r, d).wait_send()

    @pl.when(jnp.logical_and(is_helper, extra_tile % cs_n != my_at))
    def _():
        extra_copy().wait_send()

    @pl.when(extra_here)
    def _():
        extra_score_copy().wait_send()

    for q in range(blocks):
        @pl.when(jnp.logical_not(jnp.logical_or(at_home(q), skipped(q * cs_n + my_at))))
        def _():
            score_copy(q).wait_send()

    for q in range(blocks):
        here = jnp.logical_and(my_cs * blocks + q == me, me % cs_n == my_at)

        @pl.when(jnp.logical_not(here))
        def _():
            pltpu.make_async_remote_copy(
                src_ref=fin.at[0], dst_ref=ob.at[q], send_sem=score_sem.at[0],
                recv_sem=done_sem.at[q],
                device_id={"tm": me}, device_id_type=MESH).wait_recv()
        o_ref[q * rows : (q + 1) * rows, :] = ob[q]


def solution(mesh):
    group_n, tm, chan_n, sub_n = (mesh.shape[a] for a in ("groups", "tm", "chan", "sub"))
    cs_n = chan_n * sub_n
    blocks = tm // cs_n

    def on_device(traces, templates, channel_mask):
        chans, tile = traces.shape
        rows, _, span = templates.shape
        coarse = span // FINE
        wide = tile + LANES
        vmem = pl.BlockSpec(memory_space=pltpu.VMEM)
        return pl.pallas_call(
            functools.partial(kernel, (group_n, tm, chan_n, sub_n)),
            out_shape=jax.ShapeDtypeStruct((blocks * rows, tile), jnp.float32),
            in_specs=[vmem] * 3,
            out_specs=vmem,
            scratch_shapes=[
                pltpu.VMEM((tm, chans, tile), jnp.bfloat16),
                pltpu.VMEM((coarse, FINE * rows, chans), jnp.float32),
                pltpu.VMEM((FINE * rows, coarse * chans), jnp.bfloat16),
                pltpu.VMEM((coarse * chans, wide), jnp.bfloat16),
                pltpu.VMEM((FINE * rows, wide), jnp.float32),
                pltpu.VMEM((tm + 1, 2 * rows, wide), jnp.float32),
                pltpu.VMEM((rows, chans), jnp.float32),
                pltpu.VMEM(((blocks + 1) * cs_n, 2 * rows, wide), jnp.float32),
                pltpu.VMEM((blocks + 1, rows, tile), jnp.float32),
                pltpu.VMEM((blocks, rows, tile), jnp.float32),
                pltpu.VMEM((rows, chans, span), jnp.bfloat16),
                pltpu.VMEM((rows, chans), jnp.int32),
                pltpu.SemaphoreType.DMA((tm, PIECES)),
                pltpu.SemaphoreType.DMA((tm, PIECES)),
                pltpu.SemaphoreType.DMA((tm, PIECES)),
                pltpu.SemaphoreType.DMA((tm + 1,)),
                pltpu.SemaphoreType.DMA(((blocks + 1) * cs_n,)),
                pltpu.SemaphoreType.DMA((blocks + 1,)),
                pltpu.SemaphoreType.DMA((blocks,)),
                pltpu.SemaphoreType.DMA((rows,)),
                pltpu.SemaphoreType.DMA((rows,)),
                pltpu.SemaphoreType.DMA((max(group_n - 1, 1), rows)),
                pltpu.SemaphoreType.DMA,
                pltpu.SemaphoreType.DMA,
            ],
            compiler_params=pltpu.CompilerParams(collective_id=0, has_side_effects=True),
        )(traces, templates, channel_mask)

    placed = (
        P(("chan", "sub"), ("groups", "tm")),
        P("tm", ("chan", "sub"), None),
        P("tm", ("chan", "sub")),
    )
    return jax.shard_map(
        on_device,
        mesh=mesh,
        in_specs=placed,
        out_specs=P(("chan", "sub"), ("groups", "tm")),
        check_vma=False,
    )
```

time: 34 us -> 34.7 us (1.021)
  Pallas kernels: 32.4 us -> 33.1 us
    pallas_call x1, Pallas kernels: 32.4 us -> 33.1 us  [on_device(): pl.pallas_call(functools.partial(kernel, (group_n, tm, chan_n, sub_n)), o...]
where the time goes in v3:
time: 34.7 us; the launch traced here: 34.5 us
  Pallas kernels  33.1 us (95%)
  local copies, waits for them, and re-layouts  1.38 us (4%)
    pallas_call x1, Pallas kernels, on_device(): pl.pallas_call(functools.partial(kernel, (group_n, tm, chan_n, sub_n)), o...  33.1 us
    unnamed x1, local copies, waits for them, and re-layouts  1.38 us

profile of v3, /device:TPU:3, one launch (start us, length us, event | category | flops | bytes accessed | tf_op | source)
XLA Modules:
  0.0 34.5 jit_solution(2666847697849173622)
XLA Ops:
  0.0 33.1 %shard_map.37 = f32[8,1024]{1,0:T(8,128)} custom-call(bf16[128,1024]{1,0:T(8,128)(2,1)} %x_ref.1, bf16[8,128,256]{2,1,0:T(8,128)(2,1)} %w_ref.1, s32[8,128]{1,0:T(8,128)} %m_ref.1), custom_call_target="tpu_custom_call" | custom-call | tf_op jit(solution)/shard_map/pallas_call | solution.py:358
  33.1 1.4 %copy.5 = f32[8,1024]{1,0:T(8,128)} copy(f32[8,1024]{1,0:T(8,128)} %shard_map.37) | data formatting | bytes 65536

commit v4 on v2

v4 whole, which is shorter than its diff:
```python
import functools

import jax
import jax.numpy as jnp
from jax import lax
from jax.experimental import pallas as pl
from jax.experimental.pallas import tpu as pltpu
from jax.sharding import PartitionSpec as P

EPSILON = 1e-06
MESH = pl.DeviceIdType.MESH
LANES = 128
FRAMES = 4
FINE = LANES // FRAMES
PIECES = 2


def kernel(sizes, x_ref, w_ref, m_ref, o_ref, xb, af, ab, fr, pr, st, tb, rb, fin, ob,
           recv_sem, right_sem, left_sem, out_sem, in_sem, score_sem, done_sem):
    tm, chan_n, sub_n = sizes
    cs_n = chan_n * sub_n
    me = lax.axis_index("tm")
    my_chan = lax.axis_index("chan")
    my_sub = lax.axis_index("sub")
    my_cs = my_chan * sub_n + my_sub
    chans, tile = x_ref.shape
    rows, _, span = w_ref.shape
    blocks = tm // cs_n
    coarse = span // FINE
    reach = tile + LANES
    wide = tile + 2 * LANES
    owner = me // blocks
    my_at = my_sub * chan_n + my_chan

    def place(t):
        at = t % cs_n
        return at % chan_n, at // chan_n

    barrier = pltpu.get_barrier_semaphore()

    @pl.when(me < tm - 1)
    def _():
        pl.semaphore_signal(barrier, inc=1, device_id={"tm": me + 1}, device_id_type=MESH)

    @pl.when(me > 0)
    def _():
        pl.semaphore_signal(barrier, inc=1, device_id={"tm": me - 1}, device_id_type=MESH)

    for b in range(chan_n):
        for c in range(sub_n):
            if b or c:
                pl.semaphore_signal(
                    barrier, inc=1,
                    device_id={"chan": lax.rem(my_chan + b, chan_n),
                               "sub": lax.rem(my_sub + c, sub_n)},
                    device_id_type=MESH)

    xb[me] = x_ref[...]
    mask = m_ref[...].astype(jnp.float32)
    for k in range(rows):
        wave = jnp.transpose(w_ref[k].astype(jnp.float32)) * mask[k : k + 1, :]
        tb[k : k + 1, :] = jnp.sum(wave * wave, axis=0, keepdims=True)
        for g in range(coarse):
            af[g, pl.ds(k, FINE, stride=rows), :] = wave[g * FINE : (g + 1) * FINE, :]
    for g in range(coarse):
        ab[:, g * chans : (g + 1) * chans] = af[g].astype(jnp.bfloat16)
    mask_bf = mask.astype(jnp.bfloat16)
    mask_two = jnp.concatenate([mask_bf, mask_bf], 1)

    at_end = jnp.logical_or(me == 0, me == tm - 1)
    pl.semaphore_wait(barrier, cs_n - 1 + jnp.where(at_end, 1, 2))

    def relay(src, index, p, to, sem):
        columns = pl.ds(0, span) if p == 0 else pl.ds(span, tile - span)
        return pltpu.make_async_remote_copy(
            src_ref=src.at[:, columns], dst_ref=xb.at[index, :, columns],
            send_sem=sem.at[index, p], recv_sem=recv_sem.at[index, p],
            device_id={"tm": to}, device_id_type=MESH)

    for p in range(PIECES):
        @pl.when(me < tm - 1)
        def _():
            relay(x_ref, me, p, me + 1, right_sem).start()

        @pl.when(me > 0)
        def _():
            relay(x_ref, me, p, me - 1, left_sem).start()

    def sum_copy(t, kind):
        slot = (t // cs_n) * cs_n + my_cs
        to_chan, to_sub = place(t)
        part = (pl.ds(kind * rows, rows), pl.ds(0, wide if kind else tile))
        return pltpu.make_async_remote_copy(
            src_ref=st.at[(t, *part)], dst_ref=rb.at[(slot, *part)],
            send_sem=out_sem.at[t, kind], recv_sem=in_sem.at[slot, kind],
            device_id={"chan": to_chan, "sub": to_sub}, device_id_type=MESH)

    def score_copy(q):
        return pltpu.make_async_remote_copy(
            src_ref=fin.at[q], dst_ref=ob.at[me % blocks], send_sem=score_sem.at[q],
            recv_sem=done_sem.at[me % blocks],
            device_id={"tm": q * cs_n + my_at, "chan": owner // sub_n, "sub": owner % sub_n},
            device_id_type=MESH)

    def deliver(t, kind, fill):
        own = t % cs_n == my_at

        @pl.when(own)
        def _():
            fill(rb, (t // cs_n) * cs_n + my_cs)

        @pl.when(jnp.logical_not(own))
        def _():
            fill(st, t)
            sum_copy(t, kind).start()

    def process(t):
        after = lax.rem(t + 1, tm)
        ext = jnp.concatenate([xb[t], xb[after, :, :span]], 1)
        x32 = ext.astype(jnp.float32)
        square = x32 * x32
        high = square.astype(jnp.bfloat16)
        low = (square - high.astype(jnp.float32)).astype(jnp.bfloat16)
        power = jnp.dot(mask_two, jnp.concatenate([high, low], 0),
                        preferred_element_type=jnp.float32)
        by = 1
        while by < span:
            power = power + pltpu.roll(power, tile + span - by, 1)
            by *= 2

        def fill_power(ref, index):
            ref[index, rows : 2 * rows, 0:tile] = power[:, :tile]
            ref[index, rows : 2 * rows, tile : tile + LANES] = tb[...]
            ref[index, rows : 2 * rows, tile + LANES :] = mask

        deliver(t, 1, fill_power)
        ext = jnp.concatenate([ext, jnp.zeros((chans, LANES), jnp.bfloat16)], 1)
        for f in range(FRAMES):
            moved = ext[:, f * FINE : f * FINE + tile + span]
            for h in range(span // LANES):
                g = h * FRAMES + f
                fr[g * chans : (g + 1) * chans, :] = moved[:, h * LANES : h * LANES + reach]
        pr[...] = jnp.dot(ab[...], fr[...], preferred_element_type=jnp.float32)
        corr = pr[0:rows, :tile]
        for b in range(1, FINE):
            corr = corr + pltpu.roll(pr[b * rows : (b + 1) * rows, :], reach - b, 1)[:, :tile]

        def fill_corr(ref, index):
            ref[index, 0:rows, 0:tile] = corr

        deliver(t, 0, fill_corr)

    def step(u, carry):
        i = u // 2
        right_side = u % 2 == 0
        last = u == 2 * (tm - 1)
        from_left = me - 1 - i
        from_right = me + 1 + i
        for late in (False, True):
            here = jnp.logical_and(right_side != late, jnp.logical_not(last))
            for p in range(PIECES):
                if late and p == 0:
                    continue
                left_ok = jnp.logical_and(here, from_left >= 0)
                right_ok = jnp.logical_and(here, from_right <= tm - 1)
                if p:
                    left_ok = jnp.logical_and(left_ok, (me == tm - 1) == late)
                    right_ok = jnp.logical_and(right_ok, (me == 0) == late)

                @pl.when(left_ok)
                def _():
                    relay(x_ref, from_left, p, me, right_sem).wait_recv()

                    @pl.when(me < tm - 1)
                    def _():
                        relay(xb.at[from_left], from_left, p, me + 1, right_sem).start()

                @pl.when(right_ok)
                def _():
                    relay(x_ref, from_right, p, me, left_sem).wait_recv()

                    @pl.when(me > 0)
                    def _():
                        relay(xb.at[from_right], from_right, p, me - 1, left_sem).start()

        wrap = jnp.where(me == tm - 1, u == 2 * (tm - 2), last)
        t = jnp.where(wrap, tm - 1, jnp.where(right_side, me + i, from_left))
        valid = jnp.logical_or(
            wrap, jnp.logical_or(
                jnp.logical_and(jnp.logical_and(right_side, jnp.logical_not(last)),
                                from_right <= tm - 1),
                jnp.logical_and(jnp.logical_not(right_side), from_left >= 0)))

        @pl.when(valid)
        def _():
            process(t)

        return carry

    lax.fori_loop(0, 2 * (tm - 1) + 1, step, 0)

    for q in range(blocks):
        t = q * cs_n + my_at
        for c in range(cs_n):
            @pl.when(my_cs != c)
            def _():
                for kind in (1, 0):
                    part = (pl.ds(kind * rows, rows), pl.ds(0, wide if kind else tile))
                    pltpu.make_async_remote_copy(
                        src_ref=st.at[(0, *part)], dst_ref=rb.at[(q * cs_n + c, *part)],
                        send_sem=out_sem.at[0, kind], recv_sem=in_sem.at[q * cs_n + c, kind],
                        device_id={"tm": me}, device_id_type=MESH).wait_recv()

        def total(*at):
            result = rb[(q * cs_n, *at)]
            for c in range(1, cs_n):
                result = result + rb[(q * cs_n + c, *at)]
            return result

        lower, upper = slice(0, rows), slice(rows, 2 * rows)
        te = jnp.sum(total(upper, slice(tile, tile + LANES)), axis=1, keepdims=True)
        active = jnp.sum(total(upper, slice(tile + LANES, wide)), axis=1, keepdims=True)
        factor = jnp.sqrt(span * active)
        scores = (total(lower, slice(0, tile)) * factor
                  / jnp.sqrt(total(upper, slice(0, tile)) * te + EPSILON))
        here = jnp.logical_and(t == me, my_cs == owner)

        @pl.when(here)
        def _():
            ob[me % blocks] = scores

        @pl.when(jnp.logical_not(here))
        def _():
            fin[q] = scores
            score_copy(q).start()

    def finish(t, carry):
        for p in range(PIECES):
            @pl.when(jnp.logical_and(me < tm - 1, t <= me))
            def _():
                relay(x_ref, t, p, me, right_sem).wait_send()

            @pl.when(jnp.logical_and(me > 0, t >= me))
            def _():
                relay(x_ref, t, p, me, left_sem).wait_send()

        @pl.when(t % cs_n != my_at)
        def _():
            sum_copy(t, 1).wait_send()
            sum_copy(t, 0).wait_send()

        return carry

    lax.fori_loop(0, tm, finish, 0)

    for q in range(blocks):
        here = jnp.logical_and(q * cs_n + my_at == me, my_cs == owner)

        @pl.when(jnp.logical_not(here))
        def _():
            score_copy(q).wait_send()

    for q in range(blocks):
        here = jnp.logical_and(my_cs * blocks + q == me, me % cs_n == my_at)

        @pl.when(jnp.logical_not(here))
        def _():
            pltpu.make_async_remote_copy(
                src_ref=fin.at[0], dst_ref=ob.at[q], send_sem=score_sem.at[0],
                recv_sem=done_sem.at[q],
                device_id={"tm": me}, device_id_type=MESH).wait_recv()
        o_ref[q * rows : (q + 1) * rows, :] = ob[q]


def solution(mesh):
    tm, chan_n, sub_n = (mesh.shape[a] for a in ("tm", "chan", "sub"))
    cs_n = chan_n * sub_n
    blocks = tm // cs_n

    def on_device(traces, templates, channel_mask):
        chans, tile = traces.shape
        rows, _, span = templates.shape
        coarse = span // FINE
        reach = tile + LANES
        wide = tile + 2 * LANES
        vmem = pl.BlockSpec(memory_space=pltpu.VMEM)
        return pl.pallas_call(
            functools.partial(kernel, (tm, chan_n, sub_n)),
            out_shape=jax.ShapeDtypeStruct((blocks * rows, tile), jnp.float32),
            in_specs=[vmem] * 3,
            out_specs=vmem,
            scratch_shapes=[
                pltpu.VMEM((tm, chans, tile), jnp.bfloat16),
                pltpu.VMEM((coarse, FINE * rows, chans), jnp.float32),
                pltpu.VMEM((FINE * rows, coarse * chans), jnp.bfloat16),
                pltpu.VMEM((coarse * chans, reach), jnp.bfloat16),
                pltpu.VMEM((FINE * rows, reach), jnp.float32),
                pltpu.VMEM((tm, 2 * rows, wide), jnp.float32),
                pltpu.VMEM((rows, chans), jnp.float32),
                pltpu.VMEM((blocks * cs_n, 2 * rows, wide), jnp.float32),
                pltpu.VMEM((blocks, rows, tile), jnp.float32),
                pltpu.VMEM((blocks, rows, tile), jnp.float32),
                pltpu.SemaphoreType.DMA((tm, PIECES)),
                pltpu.SemaphoreType.DMA((tm, PIECES)),
                pltpu.SemaphoreType.DMA((tm, PIECES)),
                pltpu.SemaphoreType.DMA((tm, 2)),
                pltpu.SemaphoreType.DMA((blocks * cs_n, 2)),
                pltpu.SemaphoreType.DMA((blocks,)),
                pltpu.SemaphoreType.DMA((blocks,)),
            ],
            compiler_params=pltpu.CompilerParams(collective_id=0, has_side_effects=True),
        )(traces, templates, channel_mask)

    placed = (
        P(("chan", "sub"), ("groups", "tm")),
        P("tm", ("chan", "sub"), None),
        P("tm", ("chan", "sub")),
    )
    return jax.shard_map(
        on_device,
        mesh=mesh,
        in_specs=placed,
        out_specs=P(("chan", "sub"), ("groups", "tm")),
        check_vma=False,
    )
```

time: 34 us -> 34.1 us (level)
  no operation moved by 1% of the time
where the time goes in v4:
time: 34.1 us; the launch traced here: 33.9 us
  Pallas kernels  32.5 us (95%)
  local copies, waits for them, and re-layouts  1.38 us (4%)
    pallas_call x1, Pallas kernels, on_device(): pl.pallas_call(functools.partial(kernel, (tm, chan_n, sub_n)), out_shape=...  32.5 us
    unnamed x1, local copies, waits for them, and re-layouts  1.38 us

profile of v4, /device:TPU:3, one launch (start us, length us, event | category | flops | bytes accessed | tf_op | source)
XLA Modules:
  0.0 33.9 jit_solution(16777840185542413504)
XLA Ops:
  0.0 32.5 %shard_map.37 = f32[8,1024]{1,0:T(8,128)} custom-call(bf16[128,1024]{1,0:T(8,128)(2,1)} %x_ref.1, bf16[8,128,256]{2,1,0:T(8,128)(2,1)} %w_ref.1, s32[8,128]{1,0:T(8,128)} %m_ref.1), custom_call_target="tpu_custom_call" | custom-call | tf_op jit(solution)/shard_map/pallas_call | solution.py:287
  32.5 1.4 %copy.5 = f32[8,1024]{1,0:T(8,128)} copy(f32[8,1024]{1,0:T(8,128)} %shard_map.37) | data formatting | bytes 65536

commit v5 on v4

--- a/solution.py
+++ b/solution.py
@@ -30,10 +30,10 @@
     reach = tile + LANES
     wide = tile + 2 * LANES
     owner = me // blocks
-    my_at = my_sub * chan_n + my_chan
+    my_at = cs_n - 1 - (my_sub * chan_n + my_chan)
 
     def place(t):
-        at = t % cs_n
+        at = cs_n - 1 - t % cs_n
         return at % chan_n, at // chan_n
 
     barrier = pltpu.get_barrier_semaphore()

time: 34.1 us -> 33.2 us (0.974)
  the two profiles are of different devices: /device:TPU:3 before, /device:TPU:0 now
where the time goes in v5:
time: 33.2 us; the launch traced here: 33 us
  Pallas kernels  31.6 us (95%)
  local copies, waits for them, and re-layouts  1.38 us (4%)
    pallas_call x1, Pallas kernels, on_device(): pl.pallas_call(functools.partial(kernel, (tm, chan_n, sub_n)), out_shape=...  31.6 us
    unnamed x1, local copies, waits for them, and re-layouts  1.38 us

profile of v5, /device:TPU:0, one launch (start us, length us, event | category | flops | bytes accessed | tf_op | source)
XLA Modules:
  0.0 33.0 jit_solution(18044197293851283503)
XLA Ops:
  0.0 31.6 %shard_map.37 = f32[8,1024]{1,0:T(8,128)} custom-call(bf16[128,1024]{1,0:T(8,128)(2,1)} %x_ref.1, bf16[8,128,256]{2,1,0:T(8,128)(2,1)} %w_ref.1, s32[8,128]{1,0:T(8,128)} %m_ref.1), custom_call_target="tpu_custom_call" | custom-call | tf_op jit(solution)/shard_map/pallas_call | solution.py:287
  31.6 1.4 %copy.5 = f32[8,1024]{1,0:T(8,128)} copy(f32[8,1024]{1,0:T(8,128)} %shard_map.37) | data formatting | bytes 65536

commit v6 on v5

--- a/solution.py
+++ b/solution.py
@@ -201,15 +201,17 @@
 
     for q in range(blocks):
         t = q * cs_n + my_at
-        for c in range(cs_n):
-            @pl.when(my_cs != c)
-            def _():
-                for kind in (1, 0):
-                    part = (pl.ds(kind * rows, rows), pl.ds(0, wide if kind else tile))
+        def arrive(kind):
+            part = (pl.ds(kind * rows, rows), pl.ds(0, wide if kind else tile))
+            for c in range(cs_n):
+                @pl.when(my_cs != c)
+                def _():
                     pltpu.make_async_remote_copy(
                         src_ref=st.at[(0, *part)], dst_ref=rb.at[(q * cs_n + c, *part)],
                         send_sem=out_sem.at[0, kind], recv_sem=in_sem.at[q * cs_n + c, kind],
                         device_id={"tm": me}, device_id_type=MESH).wait_recv()
+
+        arrive(1)
 
         def total(*at):
             result = rb[(q * cs_n, *at)]
@@ -221,8 +223,9 @@
         te = jnp.sum(total(upper, slice(tile, tile + LANES)), axis=1, keepdims=True)
         active = jnp.sum(total(upper, slice(tile + LANES, wide)), axis=1, keepdims=True)
         factor = jnp.sqrt(span * active)
-        scores = (total(lower, slice(0, tile)) * factor
-                  / jnp.sqrt(total(upper, slice(0, tile)) * te + EPSILON))
+        root = jnp.sqrt(total(upper, slice(0, tile)) * te + EPSILON)
+        arrive(0)
+        scores = total(lower, slice(0, tile)) * factor / root
         here = jnp.logical_and(t == me, my_cs == owner)
 
         @pl.when(here)

time: 33.2 us -> 33.1 us (level)
  no operation moved by 1% of the time
where the time goes in v6:
time: 33.1 us; the launch traced here: 32.9 us
  Pallas kernels  31.5 us (95%)
  local copies, waits for them, and re-layouts  1.38 us (4%)
    pallas_call x1, Pallas kernels, on_device(): pl.pallas_call(functools.partial(kernel, (tm, chan_n, sub_n)), out_shape=...  31.5 us
    unnamed x1, local copies, waits for them, and re-layouts  1.38 us

profile of v6, /device:TPU:0, one launch (start us, length us, event | category | flops | bytes accessed | tf_op | source)
XLA Modules:
  0.0 32.9 jit_solution(11017089506030691527)
XLA Ops:
  0.0 31.5 %shard_map.37 = f32[8,1024]{1,0:T(8,128)} custom-call(bf16[128,1024]{1,0:T(8,128)(2,1)} %x_ref.1, bf16[8,128,256]{2,1,0:T(8,128)(2,1)} %w_ref.1, s32[8,128]{1,0:T(8,128)} %m_ref.1), custom_call_target="tpu_custom_call" | custom-call | tf_op jit(solution)/shard_map/pallas_call | solution.py:290
  31.5 1.4 %copy.5 = f32[8,1024]{1,0:T(8,128)} copy(f32[8,1024]{1,0:T(8,128)} %shard_map.37) | data formatting | bytes 65536
